TPU v7x, 32 devices: a whole 2x2x4 slice. The times are simulated.
32 devices in a mesh: row: 8 (over y, x, core), col: 4 (over z).
Axes of the slice: x: 2, y: 2, z: 4, core: 2. Of those that a mesh axis runs over, the one named last changes fastest.
Arguments:
- gate_input: bfloat16 [1024, 28672], P('row', 'col'), may hold values from -6 to 6
- up_input: bfloat16 [1024, 28672], P('row', 'col'), may hold values from -6 to 6
- grad_output: bfloat16 [1024, 8192], P('col', 'row'), may hold values from -0.75 to 0.75
- down_weight: bfloat16 [28672, 8192], P('col', 'row'), may hold values from -0.0625 to 0.0625
Outputs:
- grad_gate: bfloat16 [1024, 28672], P('row', 'col')
- grad_up: bfloat16 [1024, 28672], P('row', 'col')
- grad_weight: float32 [28672, 8192], P('col', 'row')
All inputs are finite; a program needn't handle non-finite values.
Results may differ from a plain program's by a relative error of at most 0.013.
Values may be sent and summed in bfloat16 or wider, within the bound.
A program may use at most 192 MiB of HBM per device.

v0:
```python
import jax
import jax.numpy as jnp
from jax import lax
from jax.sharding import PartitionSpec as P


def activation_pass(gate_input, up_input, grad_hidden):
    gate_value = gate_input.astype(jnp.float32)
    up_value = up_input.astype(jnp.float32)
    sigma = jax.nn.sigmoid(gate_value)
    swish = gate_value * sigma
    grad_up = (grad_hidden * swish).astype(jnp.bfloat16)
    grad_gate = (grad_hidden * up_value * sigma * (1.0 + gate_value * (1.0 - sigma))).astype(
        jnp.bfloat16
    )
    return (grad_gate, grad_up)


def hidden_values(gate_input, up_input):
    gate_value = gate_input.astype(jnp.float32)
    swish = gate_value * jax.nn.sigmoid(gate_value)
    return (swish * up_input.astype(jnp.float32)).astype(jnp.bfloat16)


def body(gate_input, up_input, grad_output, down_weight):
    grad_rows = lax.all_gather(grad_output, "col", axis=0, tiled=True)
    rows_block = grad_rows
    grad_hidden = lax.psum_scatter(
        lax.dot_general(
            rows_block, down_weight, (((1,), (1,)), ((), ())), preferred_element_type=jnp.float32
        ).astype(jnp.bfloat16),
        "row",
        scatter_dimension=0,
        tiled=True,
    ).astype(jnp.float32)
    grad_gate, grad_up = activation_pass(gate_input, up_input, grad_hidden)
    hidden = hidden_values(gate_input, up_input)
    rows_block = grad_rows
    grad_weight = lax.dot_general(
        lax.all_gather(hidden, "row", axis=0, tiled=True),
        rows_block,
        (((0,), (0,)), ((), ())),
        preferred_element_type=jnp.float32,
    )
    return (grad_gate, grad_up, grad_weight)


def solution(mesh):
    placed = (P("row", "col"), P("row", "col"), P("col", "row"), P("col", "row"))
    return jax.shard_map(
        body,
        mesh=mesh,
        in_specs=placed,
        out_specs=(P("row", "col"), P("row", "col"), P("col", "row")),
        check_vma=False,
    )
```

profile of v0, /device:TPU:0, one launch (start us, length us, event | category | flops | bytes accessed | tf_op | source)
XLA Modules:
  0.0 300.8 jit_solution(7648882364903081949)
XLA Ops:
  7.2 0.0 all-gather.3.cloned.1.call-start
  7.2 0.7 all-gather.3.cloned.1.call-update
  7.9 0.0 reduce-scatter.2.cloned.1.call-start
  7.9 50.3 %all-gather.3.cloned.1.call-done = bf16[1024,1024]{1,0:T(8,128)(2,1)} async-done(((bf16[256,1024]{1,0:T(8,128)(2,1)}), bf16[1024,1024]{1,0:T(8,128)(2,1)}) %all-gather.3.cloned.1.call-update) | async-done | bytes 2097168 | tf_op jit(solution)/shard_map/all_gather | solution.py:26
  58.2 22.3 %convolution_convert_fusion = bf16[1024,7168]{1,0:T(8,128)(2,1)} fusion(bf16[1024,1024]{1,0:T(8,128)(2,1)} %all-gather.3.cloned.1.call-done, bf16[7168,1024]{1,0:T(8,128)(2,1)} %param.7), kind=kOutput, calls=%fused_computation | convolution fusion | flops 15039725568 | bytes 31457280 | tf_op jit(solution)/shard_map/dot_general | solution.py:29
  80.6 0.0 copy-start
  80.6 0.0 reduce-scatter.2.cloned.1.call-update
  80.6 0.2 all-gather.5.cloned.1.call-start
  80.8 102.2 %reduce-scatter.2.cloned.1.call-done = bf16[128,7168]{1,0:T(8,128)(2,1)} async-done(((bf16[1024,7168]{1,0:T(8,128)(2,1)}), bf16[128,7168]{1,0:T(8,128)(2,1)}) %reduce-scatter.2.cloned.1.call-update) | async-done | bytes 1835024 | tf_op jit(solution)/shard_map/reduce_scatter | solution.py:28
  183.0 0.0 copy-done
  183.0 5.3 %fusion.4 = (bf16[128,7168]{1,0:T(8,128)(2,1)}, bf16[128,7168]{1,0:T(8,128)(2,1)}, bf16[128,7168]{1,0:T(8,128)(2,1)}) fusion(bf16[128,7168]{1,0:T(8,128)(2,1)S(1)} %copy-done, bf16[128,7168]{1,0:T(8,128)(2,1)} %param.4, bf16[128,7168]{1,0:T(8,128)(2,1)} %reduce-scatter.2.cloned.1.call-done), kind=kLoop, calls=%fused_computation.11 | loop fusion | flops 16515072 | bytes 11010048 | tf_op jit(solution)/shard_map/convert_element_type | solution.py:22
  188.2 0.0 all-gather.5.cloned.1.call-update
  188.3 81.1 %all-gather.5.cloned.1.call-done = bf16[1024,7168]{1,0:T(8,128)(2,1)} async-done(((bf16[128,7168]{1,0:T(8,128)(2,1)}), bf16[1024,7168]{1,0:T(8,128)(2,1)}) %all-gather.5.cloned.1.call-update) | async-done | bytes 14680080 | tf_op jit(solution)/shard_map/all_gather | solution.py:40
  269.4 24.8 %fusion.9 = f32[7168,1024]{1,0:T(8,128)} fusion(bf16[1024,7168]{1,0:T(8,128)(2,1)} %all-gather.5.cloned.1.call-done, bf16[1024,1024]{1,0:T(8,128)(2,1)} %all-gather.3.cloned.1.call-done), kind=kOutput, calls=%fused_computation.16 | convolution fusion | flops 15032385536 | bytes 46137344 | tf_op jit(solution)/shard_map/dot_general | solution.py:39
Async XLA Ops:
  7.2 51.1 %all-gather.3.cloned.1.call-start = ((), (), s32[]{:S(2)}) async-start(), calls=%async_computation.1 | async-start | bytes 2621440 | tf_op jit(solution)/shard_map/all_gather | solution.py:26
  7.9 175.1 %reduce-scatter.2.cloned.1.call-start = ((), (), s32[]{:S(2)}) async-start(), calls=%async_computation.2 | async-start | bytes 16515072 | tf_op jit(solution)/shard_map/reduce_scatter | solution.py:28
  80.6 102.4 %copy-start = (bf16[128,7168]{1,0:T(8,128)(2,1)S(1)}, bf16[128,7168]{1,0:T(8,128)(2,1)}, u32[]{:S(2)}) copy-start(bf16[128,7168]{1,0:T(8,128)(2,1)} %param.5) | copy-start | bytes 5505028
  80.6 188.8 %all-gather.5.cloned.1.call-start = ((), (), s32[]{:S(2)}) async-start(), calls=%async_computation.3 | async-start | bytes 16515072 | tf_op jit(solution)/shard_map/all_gather | solution.py:40
Sparse Core Ops, SparseCore 0:
  9.6 48.6 all-gather.2
  80.7 102.2 reduce-scatter.1
  188.4 80.9 all-gather.4
where the time goes:
time: 301 us
  waiting for transfers between devices  234 us (78%)
  matrix products  47.2 us (16%)
  between operations  13.7 us (5%)
  other arithmetic  5.25 us (2%)
    reduce_scatter x1, waiting for transfers between devices, body(): lax.psum_scatter(lax.dot_general(rows_block, down_weight, (((1,), (1,)),...  102 us
    all_gather x1, waiting for transfers between devices, body(): lax.all_gather(hidden, 'row', axis=0, tiled=True)  81.1 us
    all_gather x1, waiting for transfers between devices, body(): grad_rows = lax.all_gather(grad_output, 'col', axis=0, tiled=True)  50.3 us
    dot_general x1, matrix products, body(): lax.dot_general(lax.all_gather(hidden, 'row', axis=0, tiled=True), rows_b...  24.8 us
    dot_general x1, matrix products, body(): lax.dot_general(rows_block, down_weight, (((1,), (1,)), ((), ())), prefer...  22.3 us
  transfers between devices with their start and end apart: 3, of which 3 were waited for; matrix products, arithmetic and copies ran while one was open for 0% of the time, Pallas kernels for 0%

commit v1 on v0

v1 whole, which is shorter than its diff:
```python
import functools

import jax
import jax.numpy as jnp
from jax import lax
from jax.experimental import pallas as pl
from jax.experimental.pallas import tpu as pltpu
from jax.sharding import PartitionSpec as P

F32 = jnp.float32
BF16 = jnp.bfloat16
MESH = pl.DeviceIdType.MESH


def snake(place):
    return (place // 2) * 2 + (place + place // 2) % 2


def tile_of(width):
    return 256 if width % 256 == 0 else 128


def exchange_kernel(
    n_row, n_col, gate_ref, up_ref, go_ref, w_ref,
    hid_ref, gath_ref, gh_ref,
    hid_v, w_v, go_v, part, rs_out, rs_in, sib_out, sib_in,
    ag_ss, ag_rs, push_ss, push_rs, z_ss, z_rs, gos_ss, gos_rs, w_ss, w_rs, rs_ss, rs_rs,
    fin_ss, fin_rs, loc,
):
    me, z = lax.axis_index("row"), lax.axis_index("col")
    core, chip = me % 2, me // 2
    n = n_row // 2
    place = snake(chip)
    tok, ff = gate_ref.shape
    rows = go_ref.shape[0]
    half, quarter = ff // 2, ff // 4
    tile = tile_of(quarter)

    def row_of(ring_place):
        return snake(ring_place) * 2 + core

    sibling = (chip * 2 + 1 - core, z)
    ahead = (row_of((place + 1) % n), z)
    behind = (row_of((place + n - 1) % n), z)
    towards = (ahead, behind)
    z_peers = [(me, (z + step) % n_col) for step in range(1, n_col)]

    barrier = pltpu.get_barrier_semaphore()
    for peer in [ahead, behind, sibling] + z_peers:
        pl.semaphore_signal(barrier, inc=1, device_id=peer, device_id_type=MESH)
    pl.semaphore_wait(barrier, 3 + len(z_peers))

    sent = []

    def remote(src, dst, ss, rs, peer):
        copy = pltpu.make_async_remote_copy(
            src_ref=src, dst_ref=dst, send_sem=ss, recv_sem=rs, device_id=peer, device_id_type=MESH
        )
        copy.start()
        sent.append(copy)
        return copy

    go_here = go_v.at[core, pl.ds(z * rows, rows)]
    z_in = []
    for step, peer in enumerate(z_peers):
        z_in.append(remote(go_ref, go_here, z_ss.at[step], z_rs.at[step], peer))

    ag_in, push_in = {}, []

    def push(src_row, d, k, slot, src=None):
        span = pl.ds((2 * d + k) * quarter, quarter)
        dst = hid_ref.at[src_row, span]
        push_in.append(
            remote(dst if src is None else src, dst, push_ss.at[d, k, slot], push_rs.at[d, k, slot], sibling)
        )

    for k in range(2):
        for d in range(2):
            first = (2 * d + k) * quarter

            @pl.loop(0, quarter // tile)
            def _(j):
                span = pl.ds(pl.multiple_of(first + j * tile, 128), tile)
                gate = gate_ref[:, span].astype(F32)
                value = gate * jax.nn.sigmoid(gate) * up_ref[:, span].astype(F32)
                hid_v[span, :] = value.T.astype(BF16)

            src = hid_v.at[pl.ds(first, quarter)]
            ag_in[d, k] = remote(
                src, hid_ref.at[me, pl.ds(first, quarter)], ag_ss.at[d, k, 0], ag_rs.at[d, k, 0], towards[d]
            )

    own_go = pltpu.make_async_copy(go_ref, go_here, loc.at[0])
    own_go.start()
    go_in = [remote(go_ref, go_here, gos_ss.at[0], gos_rs.at[0], sibling)]
    w_in = remote(
        w_ref.at[pl.ds((1 - core) * half, half)], w_v.at[core], w_ss.at[0], w_rs.at[0], sibling
    )
    own_w = pltpu.make_async_copy(w_ref.at[pl.ds(core * half, half)], w_v.at[core], loc.at[1])
    own_w.start()
    for k in range(2):
        for d in range(2):
            push(me, d, k, 0, hid_v.at[pl.ds((2 * d + k) * quarter, quarter)])
    own_hid = pltpu.make_async_copy(hid_v, hid_ref.at[me], loc.at[2])
    own_hid.start()

    def arrived(step, d, k):
        ag_in[d, k].wait_recv()
        origin = (place + n - step - 1) % n if d == 0 else (place + step + 1) % n
        src_row = row_of(origin)
        if step < n - 2:
            block = hid_ref.at[src_row, pl.ds((2 * d + k) * quarter, quarter)]
            ag_in[d, k] = remote(
                block, block, ag_ss.at[d, k, step + 1], ag_rs.at[d, k, step + 1], towards[d]
            )
        push(src_row, d, k, step + 1)

    for step in range(n - 2):
        for k in range(2):
            for d in range(2):
                arrived(step, d, k)

    for step in range(n_col - 1):
        z_in[step].wait_recv()
        block = go_v.at[core, pl.ds((z + n_col - step - 1) % n_col * rows, rows)]
        go_in.append(remote(block, block, gos_ss.at[step + 1], gos_rs.at[step + 1], sibling))
    own_go.wait()
    out_go = pltpu.make_async_copy(go_v.at[core], gath_ref, loc.at[3])
    out_go.start()
    for copy in go_in:
        copy.wait_recv()
    w_in.wait_recv()
    own_w.wait()

    def partial_of(ring_place, d):
        base = pl.multiple_of(snake(ring_place) * (2 * tok), 2 * tok)

        @pl.loop(0, quarter // tile)
        def _(j):
            columns = pl.ds(pl.multiple_of(d * quarter + j * tile, 128), tile)
            total = None
            for c in range(2):
                term = lax.dot_general(
                    go_v[c, pl.ds(base, 2 * tok), :], w_v[c, columns, :],
                    (((1,), (1,)), ((), ())), preferred_element_type=F32,
                )
                total = term if total is None else total + term
            part[d, :, pl.ds(pl.multiple_of(j * tile, 128), tile)] = total

    offsets = (pl.multiple_of((1 - core) * tok, tok), pl.multiple_of(core * tok, tok))
    rs_hop = {}
    for step in range(n - 1):
        for d in range(2):
            partial_of((place + n - 1 - step) % n if d == 0 else (place + 1 + step) % n, d)
        for k in range(2):
            for d in range(2):
                if step > 0:
                    rs_hop[d, k].wait_recv()

                @pl.loop(0, quarter // tile)
                def _(j):
                    span = pl.ds(pl.multiple_of(j * tile, 128), tile)
                    value = part[d, pl.ds(offsets[k], tok), span]
                    if step > 0:
                        value = value + rs_in[d, k, step - 1, :, span].astype(F32)
                    rs_out[d, k, step, :, span] = value.astype(BF16)

                rs_hop[d, k] = remote(
                    rs_out.at[d, k, step], rs_in.at[d, k, step],
                    rs_ss.at[d, k, step], rs_rs.at[d, k, step], towards[d],
                )
        if step == 0:
            for k in range(2):
                for d in range(2):
                    arrived(n - 2, d, k)

    for d in range(2):
        partial_of(place, d)
    fin = []
    for k in range(2):
        for d in range(2):
            rs_hop[d, k].wait_recv()

            @pl.loop(0, quarter // tile)
            def _(j):
                span = pl.ds(pl.multiple_of(j * tile, 128), tile)
                value = part[d, pl.ds(offsets[k], tok), span] + rs_in[d, k, n - 2, :, span].astype(F32)
                if k == 0:
                    sib_out[d, :, span] = value.astype(BF16)
                else:
                    gh_ref[:, pl.ds(pl.multiple_of(core * half + d * quarter + j * tile, 128), tile)] = value

            if k == 0:
                fin.append(remote(sib_out.at[d], sib_in.at[d], fin_ss.at[d], fin_rs.at[d], sibling))
    for d in range(2):
        fin[d].wait_recv()

        @pl.loop(0, quarter // tile)
        def _(j):
            span = pl.ds(pl.multiple_of(j * tile, 128), tile)
            columns = pl.ds(pl.multiple_of((1 - core) * half + d * quarter + j * tile, 128), tile)
            gh_ref[:, columns] = sib_in[d, :, span].astype(F32)

    for copy in push_in:
        copy.wait_recv()
    for copy in sent:
        copy.wait_send()
    own_hid.wait()
    out_go.wait()


def exchange(n_row, n_col, gate, up, go, w):
    tok, ff = gate.shape
    rows, width = go.shape
    n = n_row // 2
    quarter = ff // 4
    dma = pltpu.SemaphoreType.DMA
    whole = pl.BlockSpec(memory_space=pltpu.VMEM)
    hbm = pl.BlockSpec(memory_space=pl.ANY)
    return pl.pallas_call(
        functools.partial(exchange_kernel, n_row, n_col),
        out_shape=(
            jax.ShapeDtypeStruct((n_row, ff, tok), BF16),
            jax.ShapeDtypeStruct((n_col * rows, width), BF16),
            jax.ShapeDtypeStruct((tok, ff), F32),
        ),
        in_specs=[whole, whole, hbm, hbm],
        out_specs=(hbm, hbm, whole),
        scratch_shapes=[
            pltpu.VMEM((ff, tok), BF16),
            pltpu.VMEM((2, ff // 2, width), BF16),
            pltpu.VMEM((2, n_col * rows, width), BF16),
            pltpu.VMEM((2, 2 * tok, quarter), F32),
            pltpu.VMEM((2, 2, n - 1, tok, quarter), BF16),
            pltpu.VMEM((2, 2, n - 1, tok, quarter), BF16),
            pltpu.VMEM((2, tok, quarter), BF16),
            pltpu.VMEM((2, tok, quarter), BF16),
            dma((2, 2, n - 1)),
            dma((2, 2, n - 1)),
            dma((2, 2, n)),
            dma((2, 2, n)),
            dma((n_col - 1,)),
            dma((n_col - 1,)),
            dma((n_col,)),
            dma((n_col,)),
            dma((1,)),
            dma((1,)),
            dma((2, 2, n - 1)),
            dma((2, 2, n - 1)),
            dma((2,)),
            dma((2,)),
            dma((4,)),
        ],
        compiler_params=pltpu.CompilerParams(
            collective_id=0, has_side_effects=True, vmem_limit_bytes=56 * 2**20
        ),
    )(gate, up, go, w)


def finish_kernel(n_row, hid_ref, go_ref, gate_ref, up_ref, gh_ref, gg_ref, gu_ref, gw_ref):
    lhs = jnp.concatenate([hid_ref[r] for r in range(n_row)], axis=1)
    gw_ref[...] = jnp.dot(lhs, go_ref[...], preferred_element_type=F32)
    gate = gate_ref[...].astype(F32)
    grad_hidden = gh_ref[...]
    sigma = jax.nn.sigmoid(gate)
    gu_ref[...] = (grad_hidden * (gate * sigma)).astype(BF16)
    gg_ref[...] = (
        grad_hidden * up_ref[...].astype(F32) * sigma * (1.0 + gate * (1.0 - sigma))
    ).astype(BF16)


def finish(hid, go, gate, up, gh):
    n_row, ff, tok = hid.shape
    tokens, width = go.shape
    tile = 512 if ff % 512 == 0 else 256
    strip = pl.BlockSpec((tok, tile), lambda j: (0, j))
    return pl.pallas_call(
        functools.partial(finish_kernel, n_row),
        grid=(ff // tile,),
        out_shape=(
            jax.ShapeDtypeStruct((tok, ff), BF16),
            jax.ShapeDtypeStruct((tok, ff), BF16),
            jax.ShapeDtypeStruct((ff, width), F32),
        ),
        in_specs=[
            pl.BlockSpec((n_row, tile, tok), lambda j: (0, j, 0)),
            pl.BlockSpec((tokens, width), lambda j: (0, 0)),
            strip, strip, strip,
        ],
        out_specs=(strip, strip, pl.BlockSpec((tile, width), lambda j: (j, 0))),
        compiler_params=pltpu.CompilerParams(vmem_limit_bytes=48 * 2**20),
    )(hid, go, gate, up, gh)


def solution(mesh):
    n_row, n_col = mesh.shape["row"], mesh.shape["col"]

    def body(gate_input, up_input, grad_output, down_weight):
        hid, go, gh = exchange(n_row, n_col, gate_input, up_input, grad_output, down_weight)
        return finish(hid, go, gate_input, up_input, gh)

    placed = (P("row", "col"), P("row", "col"), P("col", "row"), P("col", "row"))
    return jax.shard_map(
        body,
        mesh=mesh,
        in_specs=placed,
        out_specs=(P("row", "col"), P("row", "col"), P("col", "row")),
        check_vma=False,
    )
```

time: 301 us -> 161 us (0.53)
  waiting for transfers between devices: 234 us -> 0 us
  Pallas kernels: 0 us -> 158 us
  matrix products: 47.2 us -> 0 us
  between operations: 13.7 us -> 0.68 us
  other arithmetic: 5.25 us -> 0 us
    pallas_call x0 -> x2, Pallas kernels: none -> 158 us  [the longest x1 132 us: exchange(): pl.pallas_call(functools.partial(exchange_kernel, n_row, n_col), out_shap...]
    all_gather x2 -> x0, waiting for transfers between devices: 131 us -> none  [the longest x1 81.1 us: body(): lax.all_gather(hidden, 'row', axis=0, tiled=True)]
    reduce_scatter x1 -> x0, waiting for transfers between devices: 102 us -> none  [body(): lax.psum_scatter(lax.dot_general(rows_block, down_weight, (((1,), (1,)),...]
    dot_general x2 -> x0, matrix products: 47.2 us -> none  [the longest x1 24.8 us: body(): lax.dot_general(lax.all_gather(hidden, 'row', axis=0, tiled=True), rows_b...]
    convert_element_type x1 -> x0, other arithmetic: 5.25 us -> none  [hidden_values(): return (swish * up_input.astype(jnp.float32)).astype(jnp.bfloat16)]
  transfers between devices with their start and end apart: 3 -> 0, of which waited for: 3 -> 0; matrix products, arithmetic and copies ran while one was open for 0% -> 0% of each run, Pallas kernels for 0% -> 0%
where the time goes in v1:
time: 161 us; the launch traced here: 160 us
  Pallas kernels  158 us (98%)
    pallas_call x1, Pallas kernels, exchange(): pl.pallas_call(functools.partial(exchange_kernel, n_row, n_col), out_shap...  132 us
    pallas_call x1, Pallas kernels, finish(): pl.pallas_call(functools.partial(finish_kernel, n_row), grid=(ff // tile,...  26.3 us

profile of v1, /device:TPU:0, one launch (start us, length us, event | category | flops | bytes accessed | tf_op | source)
XLA Modules:
  0.0 160.4 jit_solution(16390742691086449030)
XLA Ops:
  0.6 0.0 copy-start.1
  0.6 0.0 copy-start
  0.7 131.9 %shard_map.67 = (bf16[8,7168,128]{2,1,0:T(8,128)(2,1)}, bf16[1024,1024]{1,0:T(8,128)(2,1)}, f32[128,7168]{1,0:T(8,128)}) custom-call(bf16[128,7168]{1,0:T(8,128)(2,1)} %gate_ref.3, bf16[128,7168]{1,0:T(8,128)(2,1)} %up_ref.3, bf16[256,1024]{1,0:T(8,128)(2,1)} %go_ref.1, bf16[7168,1024]{1,0:T(8,128)(2,1)} %w_ref.1), custom_call_target="tpu_custom_call" | custom-call | tf_op jit(solution)/shard_map/pallas_call | solution.py:220
  132.5 0.0 copy-done.1
  132.5 0.0 copy-done
  132.5 0.0 copy-start.2
  132.6 1.6 copy-done.2
  134.1 26.3 %shard_map.68 = (bf16[128,7168]{1,0:T(8,128)(2,1)}, bf16[128,7168]{1,0:T(8,128)(2,1)}, f32[7168,1024]{1,0:T(8,128)}) custom-call(bf16[8,7168,128]{2,1,0:T(8,128)(2,1)} %get-tuple-element.6.hid_ref, bf16[1024,1024]{1,0:T(8,128)(2,1)S(1)} %copy-done.2, bf16[128,7168]{1,0:T(8,128)(2,1)S(1)} %copy-done, bf16[128,7168]{1,0:T(8,128)(2,1)S(1)} %copy-done.1, ...), custom_call_target="tpu_custom_call" | custom-call | tf_op jit(solution)/shard_map/pallas_call | solution.py:277
Async XLA Ops:
  0.6 131.9 %copy-start.1 = (bf16[128,7168]{1,0:T(8,128)(2,1)S(1)}, bf16[128,7168]{1,0:T(8,128)(2,1)}, u32[]{:S(2)}) copy-start(bf16[128,7168]{1,0:T(8,128)(2,1)} %up_ref.3) | copy-start | bytes 5505028
  0.6 131.9 %copy-start = (bf16[128,7168]{1,0:T(8,128)(2,1)S(1)}, bf16[128,7168]{1,0:T(8,128)(2,1)}, u32[]{:S(2)}) copy-start(bf16[128,7168]{1,0:T(8,128)(2,1)} %gate_ref.3) | copy-start | bytes 5505028
  132.5 1.6 copy-start.2

commit v2 on v1

--- a/solution.py
+++ b/solution.py
@@ -22,10 +22,10 @@
 
 def exchange_kernel(
     n_row, n_col, gate_ref, up_ref, go_ref, w_ref,
-    hid_ref, gath_ref, gh_ref,
-    hid_v, w_v, go_v, part, rs_out, rs_in, sib_out, sib_in,
+    hid_ref, gath_ref, own_ref, last_ref0, last_ref1, last_ref2, last_ref3,
+    hid_v, w_v, go_v, part, own_v, rs_out, rs_in, sib_out, sib_in,
     ag_ss, ag_rs, push_ss, push_rs, z_ss, z_rs, gos_ss, gos_rs, w_ss, w_rs, rs_ss, rs_rs,
-    fin_ss, fin_rs, loc,
+    fin_ss, fin_rs, loc, last_sem,
 ):
     me, z = lax.axis_index("row"), lax.axis_index("col")
     core, chip = me % 2, me // 2
@@ -148,7 +148,23 @@
             part[d, :, pl.ds(pl.multiple_of(j * tile, 128), tile)] = total
 
     offsets = (pl.multiple_of((1 - core) * tok, tok), pl.multiple_of(core * tok, tok))
-    rs_hop = {}
+    last_refs = ((last_ref0, last_ref1), (last_ref2, last_ref3))
+    rs_hop, fin, last = {}, [], []
+
+    def own_partials():
+        for d in range(2):
+            partial_of(place, d)
+        for d in range(2):
+
+            @pl.loop(0, quarter // tile)
+            def _(j):
+                span = pl.ds(pl.multiple_of(j * tile, 128), tile)
+                sib_out[d, :, span] = part[d, pl.ds(offsets[0], tok), span].astype(BF16)
+                columns = pl.ds(pl.multiple_of(core * half + d * quarter + j * tile, 128), tile)
+                own_v[:, columns] = part[d, pl.ds(offsets[1], tok), span]
+
+            fin.append(remote(sib_out.at[d], sib_in.at[d], fin_ss.at[d], fin_rs.at[d], sibling))
+
     for step in range(n - 1):
         for d in range(2):
             partial_of((place + n - 1 - step) % n if d == 0 else (place + 1 + step) % n, d)
@@ -165,42 +181,40 @@
                         value = value + rs_in[d, k, step - 1, :, span].astype(F32)
                     rs_out[d, k, step, :, span] = value.astype(BF16)
 
-                rs_hop[d, k] = remote(
-                    rs_out.at[d, k, step], rs_in.at[d, k, step],
-                    rs_ss.at[d, k, step], rs_rs.at[d, k, step], towards[d],
-                )
+                if step < n - 2:
+                    rs_hop[d, k] = remote(
+                        rs_out.at[d, k, step], rs_in.at[d, k, step],
+                        rs_ss.at[d, k, step], rs_rs.at[d, k, step], towards[d],
+                    )
+                else:
+                    copy = pltpu.make_async_copy(
+                        rs_out.at[d, k, step], last_refs[d][k], last_sem.at[d, k]
+                    )
+                    copy.start()
+                    last.append(copy)
         if step == 0:
             for k in range(2):
                 for d in range(2):
                     arrived(n - 2, d, k)
-
-    for d in range(2):
-        partial_of(place, d)
-    fin = []
-    for k in range(2):
-        for d in range(2):
-            rs_hop[d, k].wait_recv()
-
-            @pl.loop(0, quarter // tile)
-            def _(j):
-                span = pl.ds(pl.multiple_of(j * tile, 128), tile)
-                value = part[d, pl.ds(offsets[k], tok), span] + rs_in[d, k, n - 2, :, span].astype(F32)
-                if k == 0:
-                    sib_out[d, :, span] = value.astype(BF16)
-                else:
-                    gh_ref[:, pl.ds(pl.multiple_of(core * half + d * quarter + j * tile, 128), tile)] = value
-
-            if k == 0:
-                fin.append(remote(sib_out.at[d], sib_in.at[d], fin_ss.at[d], fin_rs.at[d], sibling))
-    for d in range(2):
-        fin[d].wait_recv()
-
-        @pl.loop(0, quarter // tile)
-        def _(j):
-            span = pl.ds(pl.multiple_of(j * tile, 128), tile)
-            columns = pl.ds(pl.multiple_of((1 - core) * half + d * quarter + j * tile, 128), tile)
-            gh_ref[:, columns] = sib_in[d, :, span].astype(F32)
-
+        if step == n - 3:
+            own_partials()
+            for d in range(2):
+                fin[d].wait_recv()
+
+                @pl.loop(0, quarter // tile)
+                def _(j):
+                    span = pl.ds(pl.multiple_of(j * tile, 128), tile)
+                    columns = pl.ds(
+                        pl.multiple_of((1 - core) * half + d * quarter + j * tile, 128), tile
+                    )
+                    own_v[:, columns] = sib_in[d, :, span].astype(F32)
+
+            own_out = pltpu.make_async_copy(own_v, own_ref, loc.at[0])
+            own_out.start()
+
+    own_out.wait()
+    for copy in last:
+        copy.wait()
     for copy in push_in:
         copy.wait_recv()
     for copy in sent:
@@ -223,16 +237,18 @@
             jax.ShapeDtypeStruct((n_row, ff, tok), BF16),
             jax.ShapeDtypeStruct((n_col * rows, width), BF16),
             jax.ShapeDtypeStruct((tok, ff), F32),
-        ),
+        )
+        + (jax.ShapeDtypeStruct((tok, quarter), BF16),) * 4,
         in_specs=[whole, whole, hbm, hbm],
-        out_specs=(hbm, hbm, whole),
+        out_specs=(hbm,) * 7,
         scratch_shapes=[
             pltpu.VMEM((ff, tok), BF16),
             pltpu.VMEM((2, ff // 2, width), BF16),
             pltpu.VMEM((2, n_col * rows, width), BF16),
             pltpu.VMEM((2, 2 * tok, quarter), F32),
+            pltpu.VMEM((tok, ff), F32),
             pltpu.VMEM((2, 2, n - 1, tok, quarter), BF16),
-            pltpu.VMEM((2, 2, n - 1, tok, quarter), BF16),
+            pltpu.VMEM((2, 2, n - 2, tok, quarter), BF16),
             pltpu.VMEM((2, tok, quarter), BF16),
             pltpu.VMEM((2, tok, quarter), BF16),
             dma((2, 2, n - 1)),
@@ -245,11 +261,12 @@
             dma((n_col,)),
             dma((1,)),
             dma((1,)),
-            dma((2, 2, n - 1)),
-            dma((2, 2, n - 1)),
+            dma((2, 2, n - 2)),
+            dma((2, 2, n - 2)),
             dma((2,)),
             dma((2,)),
             dma((4,)),
+            dma((2, 2)),
         ],
         compiler_params=pltpu.CompilerParams(
             collective_id=0, has_side_effects=True, vmem_limit_bytes=56 * 2**20
@@ -257,47 +274,92 @@
     )(gate, up, go, w)
 
 
-def finish_kernel(n_row, hid_ref, go_ref, gate_ref, up_ref, gh_ref, gg_ref, gu_ref, gw_ref):
+def weight_kernel(n_row, hid_ref, go_ref, gw_ref):
     lhs = jnp.concatenate([hid_ref[r] for r in range(n_row)], axis=1)
     gw_ref[...] = jnp.dot(lhs, go_ref[...], preferred_element_type=F32)
-    gate = gate_ref[...].astype(F32)
-    grad_hidden = gh_ref[...]
-    sigma = jax.nn.sigmoid(gate)
-    gu_ref[...] = (grad_hidden * (gate * sigma)).astype(BF16)
-    gg_ref[...] = (
-        grad_hidden * up_ref[...].astype(F32) * sigma * (1.0 + gate * (1.0 - sigma))
-    ).astype(BF16)
-
-
-def finish(hid, go, gate, up, gh):
+
+
+def weight_gradient(hid, go):
     n_row, ff, tok = hid.shape
     tokens, width = go.shape
     tile = 512 if ff % 512 == 0 else 256
-    strip = pl.BlockSpec((tok, tile), lambda j: (0, j))
     return pl.pallas_call(
-        functools.partial(finish_kernel, n_row),
+        functools.partial(weight_kernel, n_row),
         grid=(ff // tile,),
-        out_shape=(
-            jax.ShapeDtypeStruct((tok, ff), BF16),
-            jax.ShapeDtypeStruct((tok, ff), BF16),
-            jax.ShapeDtypeStruct((ff, width), F32),
-        ),
+        out_shape=jax.ShapeDtypeStruct((ff, width), F32),
         in_specs=[
             pl.BlockSpec((n_row, tile, tok), lambda j: (0, j, 0)),
             pl.BlockSpec((tokens, width), lambda j: (0, 0)),
-            strip, strip, strip,
         ],
-        out_specs=(strip, strip, pl.BlockSpec((tile, width), lambda j: (j, 0))),
-        compiler_params=pltpu.CompilerParams(vmem_limit_bytes=48 * 2**20),
-    )(hid, go, gate, up, gh)
+        out_specs=pl.BlockSpec((tile, width), lambda j: (j, 0)),
+        cost_estimate=pl.CostEstimate(
+            flops=2 * ff * tokens * width,
+            bytes_accessed=2 * ff * tokens + 2 * tokens * width + 4 * ff * width,
+            transcendentals=0,
+        ),
+        compiler_params=pltpu.CompilerParams(vmem_limit_bytes=58 * 2**20),
+    )(hid, go)
+
+
+def activation_kernel(core_ref, r0, r1, r2, r3, own_ref, gate_ref, up_ref, gg_ref, gu_ref):
+    step = pl.program_id(0)
+    for index, sums in enumerate((r0, r1, r2, r3)):
+
+        @pl.when(step == index)
+        def _():
+            gate = gate_ref[...].astype(F32)
+            grad_hidden = own_ref[...] + sums[0].astype(F32)
+            sigma = jax.nn.sigmoid(gate)
+            gu_ref[...] = (grad_hidden * (gate * sigma)).astype(BF16)
+            gg_ref[...] = (
+                grad_hidden * up_ref[...].astype(F32) * sigma * (1.0 + gate * (1.0 - sigma))
+            ).astype(BF16)
+
+
+def activation_pass(core, sums, own, gate, up):
+    tok, ff = gate.shape
+    quarter = ff // 4
+
+    def strip_at(step, core_ref):
+        k, d = step // 2, step % 2
+        owner = k * core_ref[0] + (1 - k) * (1 - core_ref[0])
+        return (0, owner * 2 + d)
+
+    strip = pl.BlockSpec((tok, quarter), strip_at)
+    whole = pl.BlockSpec((1, tok, quarter), lambda step, core_ref: (0, 0, 0))
+    return pl.pallas_call(
+        activation_kernel,
+        out_shape=(jax.ShapeDtypeStruct((tok, ff), BF16),) * 2,
+        grid_spec=pltpu.PrefetchScalarGridSpec(
+            num_scalar_prefetch=1,
+            grid=(4,),
+            in_specs=[whole] * 4 + [strip] * 3,
+            out_specs=(strip, strip),
+        ),
+        compiler_params=pltpu.CompilerParams(vmem_limit_bytes=58 * 2**20),
+    )(core, *[s[None] for s in sums], own, gate, up)
 
 
 def solution(mesh):
     n_row, n_col = mesh.shape["row"], mesh.shape["col"]
+    n = n_row // 2
+
+    def last_hop(value, d, k):
+        move = 1 if d == 0 else n - 1
+        pairs = [
+            (snake(p) * 2 + c, snake((p + move) % n) * 2 + (c if k == 1 else 1 - c))
+            for p in range(n)
+            for c in range(2)
+        ]
+        return lax.ppermute(value, "row", pairs)
 
     def body(gate_input, up_input, grad_output, down_weight):
-        hid, go, gh = exchange(n_row, n_col, gate_input, up_input, grad_output, down_weight)
-        return finish(hid, go, gate_input, up_input, gh)
+        hid, go, own, *last = exchange(n_row, n_col, gate_input, up_input, grad_output, down_weight)
+        sums = [last_hop(last[2 * d + k], d, k) for k in range(2) for d in range(2)]
+        grad_weight = weight_gradient(hid, go)
+        core = (lax.axis_index("row") % 2).astype(jnp.int32).reshape(1)
+        grad_gate, grad_up = activation_pass(core, sums, own, gate_input, up_input)
+        return grad_gate, grad_up, grad_weight
 
     placed = (P("row", "col"), P("row", "col"), P("col", "row"), P("col", "row"))
     return jax.shard_map(

time: 161 us -> 150 us (0.932)
  Pallas kernels: 158 us -> 143 us
  starting transfers between devices: 0 us -> 3.82 us
    pallas_call x1, Pallas kernels: 132 us -> 111 us  [exchange(): pl.pallas_call(functools.partial(exchange_kernel, n_row, n_col), out_shap...]
    pallas_call x1 -> x2, Pallas kernels: 26.3 us -> 32.6 us  [the longest x1 25.7 us: weight_gradient(): pl.pallas_call(functools.partial(weight_kernel, n_row), grid=(ff // tile,...]
    ppermute x0 -> x4, starting transfers between devices: none -> 3.82 us  [last_hop(): return lax.ppermute(value, 'row', pairs)]
  transfers between devices with their start and end apart: 0 -> 4, of which waited for: 0 -> 0; matrix products, arithmetic and copies ran while one was open for 0% -> 0% of each run, Pallas kernels for 0% -> 17%
where the time goes in v2:
time: 150 us; the launch traced here: 149 us
  Pallas kernels  143 us (95%)
  starting transfers between devices  3.82 us (3%)
    pallas_call x1, Pallas kernels, exchange(): pl.pallas_call(functools.partial(exchange_kernel, n_row, n_col), out_shap...  111 us
    pallas_call x1, Pallas kernels, weight_gradient(): pl.pallas_call(functools.partial(weight_kernel, n_row), grid=(ff // tile,...  25.7 us
    pallas_call x1, Pallas kernels, activation_pass(): pl.pallas_call(activation_kernel, out_shape=(jax.ShapeDtypeStruct((tok, f...  6.84 us
    ppermute x4, starting transfers between devices, last_hop(): return lax.ppermute(value, 'row', pairs)  3.82 us
  transfers between devices with their start and end apart: 4, of which 0 were waited for; matrix products, arithmetic and copies ran while one was open for 0% of the time, Pallas kernels for 17%

profile of v2, /device:TPU:0, one launch (start us, length us, event | category | flops | bytes accessed | tf_op | source)
XLA Modules:
  0.0 149.1 jit_solution(13784348491793102531)
XLA Ops:
  0.6 110.8 %shard_map.67 = (bf16[8,7168,128]{2,1,0:T(8,128)(2,1)}, bf16[1024,1024]{1,0:T(8,128)(2,1)}, f32[128,7168]{1,0:T(8,128)}, bf16[128,1792]{1,0:T(8,128)(2,1)}, bf16...) custom-call(bf16[128,7168]{1,0:T(8,128)(2,1)} %gate_ref.3, bf16[128,7168]{1,0:T(8,128)(2,1)} %up_ref.3, ...), custom_call_target="tpu_custom_call" | custom-call | tf_op jit(solution)/shard_map/pallas_call | solution.py:234
  111.4 0.1 collective-permute-start
  111.6 1.7 %collective-permute-start.1 = (bf16[128,1792]{1,0:T(8,128)(2,1)}, bf16[128,1792]{1,0:T(8,128)(2,1)S(1)}, u32[]{:S(2)}, u32[]{:S(2)}) collective-permute-start(bf16[128,1792]{1,0:T(8,128)(2,1)} %get-tuple-element.13), channel_id=1, source_target_pairs={{0,20},{4,16},{8,4},{12,0},{24,12},{28,8},{16,28},{20,24},{1,21},{... | collective-permute-start | bytes 1376264 | tf_op jit(solution)/shard_map/ppermute | solution.py:354
  113.2 1.5 %collective-permute-start.2 = (bf16[128,1792]{1,0:T(8,128)(2,1)}, bf16[128,1792]{1,0:T(8,128)(2,1)S(1)}, u32[]{:S(2)}, u32[]{:S(2)}) collective-permute-start(bf16[128,1792]{1,0:T(8,128)(2,1)} %get-tuple-element.14), channel_id=1, source_target_pairs={{0,8},{4,12},{8,24},{12,28},{24,16},{28,20},{16,0},{20,4},{1,9},{5... | collective-permute-start | bytes 1376264 | tf_op jit(solution)/shard_map/ppermute | solution.py:354
  114.8 0.5 collective-permute-start.3
  115.3 25.7 %shard_map.69 = f32[7168,1024]{1,0:T(8,128)} custom-call(bf16[8,7168,128]{2,1,0:T(8,128)(2,1)} %get-tuple-element.19.hid_ref, bf16[1024,1024]{1,0:T(8,128)(2,1)} %get-tuple-element.20.go_ref), custom_call_target="tpu_custom_call" | custom-call | flops 15032385536 | bytes 46137344 | tf_op jit(solution)/shard_map/pallas_call | solution.py:286
  141.0 0.0 collective-permute-done
  141.0 0.0 copy-start
  141.0 0.0 collective-permute-done.1
  141.0 0.0 copy-start.1
  141.0 0.0 collective-permute-done.2
  141.0 0.0 copy-start.2
  141.0 0.0 collective-permute-done.3
  141.0 0.0 copy-start.3
  141.0 0.7 copy-done
  141.7 0.2 copy-done.1
  141.9 0.2 copy-done.2
  142.1 0.1 copy-done.3
  142.2 6.8 %shard_map.68 = (bf16[128,7168]{1,0:T(8,128)(2,1)}, bf16[128,7168]{1,0:T(8,128)(2,1)}) custom-call(s32[1]{0:T(128)} %bitcast.core_ref, bf16[1,128,1792]{2,1,0:T(8,128)(2,1)} %bitcast.5, bf16[1,128,1792]{2,1,0:T(8,128)(2,1)} %bitcast.6, bf16[1,128,1792]{2,1,0:T(8,128)(2,1)} %bitcast.7, bf16[1,128,1792]{2,1,0:T(8,128)(2,1)} %bitcast.8, ...), custom_call_target="tpu_custom_call" | custom-call | tf_op jit(solution)/shard_map/pallas_call | solution.py:330
Async XLA Ops:
  111.4 29.6 %collective-permute-start = (bf16[128,1792]{1,0:T(8,128)(2,1)}, bf16[128,1792]{1,0:T(8,128)(2,1)S(1)}, u32[]{:S(2)}, u32[]{:S(2)}) collective-permute-start(bf16[128,1792]{1,0:T(8,128)(2,1)} %get-tuple-element.12), channel_id=1, source_target_pairs={{0,12},{4,8},{8,28},{12,24},{24,20},{28,16},{16,4},{20,0},{1,13},{... | collective-permute-start | bytes 1376264 | tf_op jit(solution)/shard_map/ppermute | solution.py:354
  111.6 29.4 %collective-permute-start.1 = (bf16[128,1792]{1,0:T(8,128)(2,1)}, bf16[128,1792]{1,0:T(8,128)(2,1)S(1)}, u32[]{:S(2)}, u32[]{:S(2)}) collective-permute-start(bf16[128,1792]{1,0:T(8,128)(2,1)} %get-tuple-element.13), channel_id=1, source_target_pairs={{0,20},{4,16},{8,4},{12,0},{24,12},{28,8},{16,28},{20,24},{1,21},{... | collective-permute-start | bytes 1376264 | tf_op jit(solution)/shard_map/ppermute | solution.py:354
  113.2 27.8 %collective-permute-start.2 = (bf16[128,1792]{1,0:T(8,128)(2,1)}, bf16[128,1792]{1,0:T(8,128)(2,1)S(1)}, u32[]{:S(2)}, u32[]{:S(2)}) collective-permute-start(bf16[128,1792]{1,0:T(8,128)(2,1)} %get-tuple-element.14), channel_id=1, source_target_pairs={{0,8},{4,12},{8,24},{12,28},{24,16},{28,20},{16,0},{20,4},{1,9},{5... | collective-permute-start | bytes 1376264 | tf_op jit(solution)/shard_map/ppermute | solution.py:354
  114.8 26.3 %collective-permute-start.3 = (bf16[128,1792]{1,0:T(8,128)(2,1)}, bf16[128,1792]{1,0:T(8,128)(2,1)S(1)}, u32[]{:S(2)}, u32[]{:S(2)}) collective-permute-start(bf16[128,1792]{1,0:T(8,128)(2,1)} %get-tuple-element.15), channel_id=1, source_target_pairs={{0,16},{4,20},{8,0},{12,4},{24,8},{28,12},{16,24},{20,28},{1,17},{... | collective-permute-start | bytes 1376264 | tf_op jit(solution)/shard_map/ppermute | solution.py:354
  141.0 0.8 copy-start
  141.0 0.9 copy-start.1
  141.0 1.1 copy-start.2
  141.0 1.2 copy-start.3

commit v3 on v2

--- a/solution.py
+++ b/solution.py
@@ -74,21 +74,27 @@
             remote(dst if src is None else src, dst, push_ss.at[d, k, slot], push_rs.at[d, k, slot], sibling)
         )
 
-    for k in range(2):
-        for d in range(2):
-            first = (2 * d + k) * quarter
-
-            @pl.loop(0, quarter // tile)
-            def _(j):
-                span = pl.ds(pl.multiple_of(first + j * tile, 128), tile)
-                gate = gate_ref[:, span].astype(F32)
-                value = gate * jax.nn.sigmoid(gate) * up_ref[:, span].astype(F32)
-                hid_v[span, :] = value.T.astype(BF16)
-
-            src = hid_v.at[pl.ds(first, quarter)]
-            ag_in[d, k] = remote(
-                src, hid_ref.at[me, pl.ds(first, quarter)], ag_ss.at[d, k, 0], ag_rs.at[d, k, 0], towards[d]
-            )
+    def hidden_quarter(d, k):
+        first = (2 * d + k) * quarter
+
+        @pl.loop(0, quarter // tile)
+        def _(j):
+            span = pl.ds(pl.multiple_of(first + j * tile, 128), tile)
+            gate = gate_ref[:, span].astype(F32)
+            value = gate * jax.nn.sigmoid(gate) * up_ref[:, span].astype(F32)
+            hid_v[span, :] = value.T.astype(BF16)
+
+    def first_hop(d, k):
+        span = pl.ds((2 * d + k) * quarter, quarter)
+        ag_in[d, k] = remote(
+            hid_v.at[span], hid_ref.at[me, span], ag_ss.at[d, k, 0], ag_rs.at[d, k, 0], towards[d]
+        )
+
+    for d in range(2):
+        hidden_quarter(d, 0)
+        first_hop(d, 0)
+    for d in range(2):
+        hidden_quarter(d, 1)
 
     own_go = pltpu.make_async_copy(go_ref, go_here, loc.at[0])
     own_go.start()
@@ -103,6 +109,10 @@
             push(me, d, k, 0, hid_v.at[pl.ds((2 * d + k) * quarter, quarter)])
     own_hid = pltpu.make_async_copy(hid_v, hid_ref.at[me], loc.at[2])
     own_hid.start()
+    for d in range(2):
+        ag_in[d, 0].wait_send()
+        sent[:] = [copy for copy in sent if copy is not ag_in[d, 0]]
+        first_hop(d, 1)
 
     def arrived(step, d, k):
         ag_in[d, k].wait_recv()
@@ -165,34 +175,52 @@
 
             fin.append(remote(sib_out.at[d], sib_in.at[d], fin_ss.at[d], fin_rs.at[d], sibling))
 
+    def round_out(step, d, k):
+        if step > 0:
+            rs_hop[d, k].wait_recv()
+
+        @pl.loop(0, quarter // tile)
+        def _(j):
+            span = pl.ds(pl.multiple_of(j * tile, 128), tile)
+            value = part[d, pl.ds(offsets[k], tok), span]
+            if step > 0:
+                value = value + rs_in[d, k, step - 1, :, span].astype(F32)
+            rs_out[d, k, step, :, span] = value.astype(BF16)
+
+    def send_out(step, d, k):
+        if step < n - 2:
+            rs_hop[d, k] = remote(
+                rs_out.at[d, k, step], rs_in.at[d, k, step],
+                rs_ss.at[d, k, step], rs_rs.at[d, k, step], towards[d],
+            )
+        else:
+            copy = pltpu.make_async_copy(rs_out.at[d, k, step], last_refs[d][k], last_sem.at[d, k])
+            copy.start()
+            last.append(copy)
+
+    def partial_at(step, d):
+        partial_of((place + n - 1 - step) % n if d == 0 else (place + 1 + step) % n, d)
+
+    for d in range(2):
+        partial_at(0, d)
+        round_out(0, d, 0)
+        send_out(0, d, 0)
+        round_out(0, d, 1)
     for step in range(n - 1):
-        for d in range(2):
-            partial_of((place + n - 1 - step) % n if d == 0 else (place + 1 + step) % n, d)
-        for k in range(2):
+        if step == 0:
+            partial_at(1, 0)
             for d in range(2):
-                if step > 0:
-                    rs_hop[d, k].wait_recv()
-
-                @pl.loop(0, quarter // tile)
-                def _(j):
-                    span = pl.ds(pl.multiple_of(j * tile, 128), tile)
-                    value = part[d, pl.ds(offsets[k], tok), span]
-                    if step > 0:
-                        value = value + rs_in[d, k, step - 1, :, span].astype(F32)
-                    rs_out[d, k, step, :, span] = value.astype(BF16)
-
-                if step < n - 2:
-                    rs_hop[d, k] = remote(
-                        rs_out.at[d, k, step], rs_in.at[d, k, step],
-                        rs_ss.at[d, k, step], rs_rs.at[d, k, step], towards[d],
-                    )
-                else:
-                    copy = pltpu.make_async_copy(
-                        rs_out.at[d, k, step], last_refs[d][k], last_sem.at[d, k]
-                    )
-                    copy.start()
-                    last.append(copy)
-        if step == 0:
+                send_out(0, d, 1)
+            partial_at(1, 1)
+        else:
+            if step > 1:
+                for d in range(2):
+                    partial_at(step, d)
+            for k in range(2):
+                for d in range(2):
+                    round_out(step, d, k)
+                    send_out(step, d, k)
+        if step == 1:
             for k in range(2):
                 for d in range(2):
                     arrived(n - 2, d, k)
@@ -282,7 +310,7 @@
 def weight_gradient(hid, go):
     n_row, ff, tok = hid.shape
     tokens, width = go.shape
-    tile = 512 if ff % 512 == 0 else 256
+    tile = next(t for t in (1792, 1024, 512, 256) if ff % t == 0)
     return pl.pallas_call(
         functools.partial(weight_kernel, n_row),
         grid=(ff // tile,),
@@ -297,7 +325,7 @@
             bytes_accessed=2 * ff * tokens + 2 * tokens * width + 4 * ff * width,
             transcendentals=0,
         ),
-        compiler_params=pltpu.CompilerParams(vmem_limit_bytes=58 * 2**20),
+        compiler_params=pltpu.CompilerParams(vmem_limit_bytes=50 * 2**20),
     )(hid, go)
 
 
@@ -336,7 +364,7 @@
             in_specs=[whole] * 4 + [strip] * 3,
             out_specs=(strip, strip),
         ),
-        compiler_params=pltpu.CompilerParams(vmem_limit_bytes=58 * 2**20),
+        compiler_params=pltpu.CompilerParams(vmem_limit_bytes=48 * 2**20),
     )(core, *[s[None] for s in sums], own, gate, up)
 
 

time: 150 us -> 146 us (0.973)
  Pallas kernels: 143 us -> 138 us
  local copies, waits for them, and re-layouts: 1.19 us -> 3.09 us
    pallas_call x1, Pallas kernels: 25.7 us -> 22 us  [weight_gradient(): pl.pallas_call(functools.partial(weight_kernel, n_row), grid=(ff // tile,...]
    unnamed x8 -> x6, local copies, waits for them, and re-layouts: 1.19 us -> 3.09 us
  transfers between devices with their start and end apart: 4 -> 4, of which waited for: 0 -> 0; matrix products, arithmetic and copies ran while one was open for 0% -> 0% of each run, Pallas kernels for 17% -> 15%
where the time goes in v3:
time: 146 us
  Pallas kernels  138 us (95%)
  starting transfers between devices  3.82 us (3%)
  local copies, waits for them, and re-layouts  3.09 us (2%)
    pallas_call x1, Pallas kernels, exchange(): pl.pallas_call(functools.partial(exchange_kernel, n_row, n_col), out_shap...  111 us
    pallas_call x1, Pallas kernels, weight_gradient(): pl.pallas_call(functools.partial(weight_kernel, n_row), grid=(ff // tile,...  22 us
    pallas_call x1, Pallas kernels, activation_pass(): pl.pallas_call(activation_kernel, out_shape=(jax.ShapeDtypeStruct((tok, f...  5.54 us
    ppermute x4, starting transfers between devices, last_hop(): return lax.ppermute(value, 'row', pairs)  3.82 us
    unnamed x6, local copies, waits for them, and re-layouts  3.09 us
  transfers between devices with their start and end apart: 4, of which 0 were waited for; matrix products, arithmetic and copies ran while one was open for 0% of the time, Pallas kernels for 15%

profile of v3, /device:TPU:0, one launch (start us, length us, event | category | flops | bytes accessed | tf_op | source)
XLA Modules:
  0.0 145.9 jit_solution(11442250087963952481)
XLA Ops:
  0.6 110.8 %shard_map.67 = (bf16[8,7168,128]{2,1,0:T(8,128)(2,1)}, bf16[1024,1024]{1,0:T(8,128)(2,1)}, f32[128,7168]{1,0:T(8,128)}, bf16[128,1792]{1,0:T(8,128)(2,1)}, bf16...) custom-call(bf16[128,7168]{1,0:T(8,128)(2,1)} %gate_ref.3, bf16[128,7168]{1,0:T(8,128)(2,1)} %up_ref.3, ...), custom_call_target="tpu_custom_call" | custom-call | tf_op jit(solution)/shard_map/pallas_call | solution.py:262
  111.4 0.1 collective-permute-start
  111.5 1.7 %collective-permute-start.1 = (bf16[128,1792]{1,0:T(8,128)(2,1)}, bf16[128,1792]{1,0:T(8,128)(2,1)S(1)}, u32[]{:S(2)}, u32[]{:S(2)}) collective-permute-start(bf16[128,1792]{1,0:T(8,128)(2,1)} %get-tuple-element.13), channel_id=1, source_target_pairs={{0,20},{4,16},{8,4},{12,0},{24,12},{28,8},{16,28},{20,24},{1,21},{... | collective-permute-start | bytes 1376264 | tf_op jit(solution)/shard_map/ppermute | solution.py:382
  113.2 1.5 %collective-permute-start.2 = (bf16[128,1792]{1,0:T(8,128)(2,1)}, bf16[128,1792]{1,0:T(8,128)(2,1)S(1)}, u32[]{:S(2)}, u32[]{:S(2)}) collective-permute-start(bf16[128,1792]{1,0:T(8,128)(2,1)} %get-tuple-element.14), channel_id=1, source_target_pairs={{0,8},{4,12},{8,24},{12,28},{24,16},{28,20},{16,0},{20,4},{1,9},{5... | collective-permute-start | bytes 1376264 | tf_op jit(solution)/shard_map/ppermute | solution.py:382
  114.8 0.5 collective-permute-start.3
  115.3 0.0 copy-start.2
  115.3 1.6 %copy-done.2 = bf16[1024,1024]{1,0:T(8,128)(2,1)S(1)} copy-done((bf16[1024,1024]{1,0:T(8,128)(2,1)S(1)}, bf16[1024,1024]{1,0:T(8,128)(2,1)}, u32[]{:S(2)}) %copy-start.2) | copy-done | bytes 2097176
  116.9 0.0 copy-start
  116.9 22.0 %shard_map.69 = f32[7168,1024]{1,0:T(8,128)} custom-call(bf16[8,7168,128]{2,1,0:T(8,128)(2,1)} %get-tuple-element.19.hid_ref, bf16[1024,1024]{1,0:T(8,128)(2,1)S(1)} %copy-done.2), custom_call_target="tpu_custom_call" | custom-call | flops 15032385536 | bytes 46137344 | tf_op jit(solution)/shard_map/pallas_call | solution.py:314
  138.9 0.0 collective-permute-done
  138.9 0.0 collective-permute-done.1
  138.9 0.0 collective-permute-done.2
  138.9 0.0 collective-permute-done.3
  138.9 0.0 copy-done
  138.9 0.0 copy-start.1
  138.9 1.5 %copy-done.1 = bf16[128,7168]{1,0:T(8,128)(2,1)S(1)} copy-done((bf16[128,7168]{1,0:T(8,128)(2,1)S(1)}, bf16[128,7168]{1,0:T(8,128)(2,1)}, u32[]{:S(2)}) %copy-start.1) | copy-done | bytes 1835032
  140.4 5.5 %shard_map.68 = (bf16[128,7168]{1,0:T(8,128)(2,1)}, bf16[128,7168]{1,0:T(8,128)(2,1)}) custom-call(s32[1]{0:T(128)} %bitcast.core_ref, bf16[1,128,1792]{2,1,0:T(8,128)(2,1)S(1)} %bitcast.5, bf16[1,128,1792]{2,1,0:T(8,128)(2,1)S(1)} %bitcast.6, bf16[1,128,1792]{2,1,0:T(8,128)(2,1)S(1)} %bitcast.7, bf16[1,128,1792]{2,1,0:T(8,128)(2,1)} %bitcast.4.r3, ...), custom_call_target="tpu_custom_call" | custom-call | tf_op jit(solution)/shard_map/pallas_call | solution.py:358
Async XLA Ops:
  111.4 27.4 %collective-permute-start = (bf16[128,1792]{1,0:T(8,128)(2,1)}, bf16[128,1792]{1,0:T(8,128)(2,1)S(1)}, u32[]{:S(2)}, u32[]{:S(2)}) collective-permute-start(bf16[128,1792]{1,0:T(8,128)(2,1)} %get-tuple-element.12), channel_id=1, source_target_pairs={{0,12},{4,8},{8,28},{12,24},{24,20},{28,16},{16,4},{20,0},{1,13},{... | collective-permute-start | bytes 1376264 | tf_op jit(solution)/shard_map/ppermute | solution.py:382
  111.5 27.4 %collective-permute-start.1 = (bf16[128,1792]{1,0:T(8,128)(2,1)}, bf16[128,1792]{1,0:T(8,128)(2,1)S(1)}, u32[]{:S(2)}, u32[]{:S(2)}) collective-permute-start(bf16[128,1792]{1,0:T(8,128)(2,1)} %get-tuple-element.13), channel_id=1, source_target_pairs={{0,20},{4,16},{8,4},{12,0},{24,12},{28,8},{16,28},{20,24},{1,21},{... | collective-permute-start | bytes 1376264 | tf_op jit(solution)/shard_map/ppermute | solution.py:382
  113.2 25.6 %collective-permute-start.2 = (bf16[128,1792]{1,0:T(8,128)(2,1)}, bf16[128,1792]{1,0:T(8,128)(2,1)S(1)}, u32[]{:S(2)}, u32[]{:S(2)}) collective-permute-start(bf16[128,1792]{1,0:T(8,128)(2,1)} %get-tuple-element.14), channel_id=1, source_target_pairs={{0,8},{4,12},{8,24},{12,28},{24,16},{28,20},{16,0},{20,4},{1,9},{5... | collective-permute-start | bytes 1376264 | tf_op jit(solution)/shard_map/ppermute | solution.py:382
  114.8 24.1 %collective-permute-start.3 = (bf16[128,1792]{1,0:T(8,128)(2,1)}, bf16[128,1792]{1,0:T(8,128)(2,1)}, u32[]{:S(2)}, u32[]{:S(2)}) collective-permute-start(bf16[128,1792]{1,0:T(8,128)(2,1)} %get-tuple-element.15), channel_id=1, source_target_pairs={{0,16},{4,20},{8,0},{12,4},{24,8},{28,12},{16,24},{20,28},{1,17},{... | collective-permute-start | bytes 1376264 | tf_op jit(solution)/shard_map/ppermute | solution.py:382
  115.3 1.6 %copy-start.2 = (bf16[1024,1024]{1,0:T(8,128)(2,1)S(1)}, bf16[1024,1024]{1,0:T(8,128)(2,1)}, u32[]{:S(2)}) copy-start(bf16[1024,1024]{1,0:T(8,128)(2,1)} %get-tuple-element.20.go_ref) | copy-start | bytes 6291460
  116.9 22.0 %copy-start = (bf16[128,7168]{1,0:T(8,128)(2,1)S(1)}, bf16[128,7168]{1,0:T(8,128)(2,1)}, u32[]{:S(2)}) copy-start(bf16[128,7168]{1,0:T(8,128)(2,1)} %gate_ref.3) | copy-start | bytes 5505028
  138.9 1.5 %copy-start.1 = (bf16[128,7168]{1,0:T(8,128)(2,1)S(1)}, bf16[128,7168]{1,0:T(8,128)(2,1)}, u32[]{:S(2)}) copy-start(bf16[128,7168]{1,0:T(8,128)(2,1)} %up_ref.3) | copy-start | bytes 5505028
